TPU v7x, 256 devices: a whole 4x4x8 slice. The times are simulated.
256 devices in a mesh: lat: 16 (over y_lo, x, core), lon: 16 (over y_hi, z).
Axes of the slice: x: 4, y: 4 (y_hi: 2, y_lo: 2; y = y_hi * 2 + y_lo), z: 8, core: 2. Of those that a mesh axis runs over, the one named last changes fastest.
Arguments:
- state: bfloat16 [64, 128, 4320], P(None, 'lat', 'lon'), may hold values from -6 to 6
- land_sea: int32 [128, 4320], P('lat', 'lon'), may hold values 0 or 1
- cotangent: bfloat16 [64, 128, 4320], P(None, 'lat', 'lon'), may hold values from -6 to 6
- kernel: float32 [64, 7, 7], replicated, may hold values from -0.875 to 0.875
- conv_bias: float32 [64], replicated, may hold values from -4 to 4
- ln_gain: float32 [64], replicated, may hold values from 0.1 to 1.9
- ln_bias: float32 [64], replicated, may hold values from -3 to 3
- w_expand: bfloat16 [64, 256], replicated, may hold values from -0.75 to 0.75
- b_expand: float32 [256], replicated, may hold values from -3 to 3
- w_project: bfloat16 [256, 64], replicated, may hold values from -0.375 to 0.375
Outputs:
- state_grad: bfloat16 [64, 128, 4320], P(None, 'lat', 'lon')
- kernel_grad: float32 [64, 7, 7], replicated
- conv_bias_grad: float32 [64], replicated
- gain_grad: float32 [64], replicated
- ln_bias_grad: float32 [64], replicated
- expand_grad: float32 [64, 256], replicated
- b_expand_grad: float32 [256], replicated
- project_grad: float32 [256, 64], replicated
- b_project_grad: float32 [64], replicated
Inputs may be any that keep to these rules, and one draw needn't show every extreme that they name: `land_sea`: 1 marks an ocean cell, 0 a land cell.
All inputs are finite; a program needn't handle non-finite values. No bound on the sum of `land_sea` on one device may be relied on, other than what follows from the above.
Results may differ from a plain program's by a relative error of at most 0.0064.
Values may be sent and summed in bfloat16 or wider, within the bound.
A program may use at most 64 MiB of HBM per device.

v0:
```python
import math

import jax
import jax.numpy as jnp
from jax import lax
from jax.experimental import pallas as pl
from jax.experimental.pallas import tpu as pltpu
from jax.sharding import PartitionSpec as P

TAPS = 7
CHAN = 64
EXPAND = 256
ROWS = 8
COLS = 270
HALF = 135
PITCH = 136
TILES = 17
CELLS = ROWS * PITCH
EXT_ROWS = 14
EXT_COLS = 144
STEP = 272
PART = 1088
GROUP = 272
BACK = 1088
UA = 3
UB = 5
UE = 2
N_GROUP = 16
MESH = pl.DeviceIdType.MESH

ln_eps = 1e-06
root_half = 0.7071067811865476
inv_root_tau = 0.3989422804014327
half_log2e = -0.7213475204444817

f32 = jnp.float32
bf16 = jnp.bfloat16


def dot(a, b, dims):
    return lax.dot_general(a, b, (dims, ((), ())), preferred_element_type=f32)


NN = ((1,), (0,))
NT = ((1,), (1,))
TN = ((0,), (0,))


def split(x):
    hi = x.astype(bf16)
    lo = (x - hi.astype(f32)).astype(bf16)
    return jnp.concatenate([hi, lo], axis=1)


def kernel_body(
    state_hbm,
    cot_hbm,
    land_hbm,
    kern_hbm,
    cb_hbm,
    gain_hbm,
    lb_hbm,
    we_hbm,
    be_hbm,
    wp_hbm,
    grad_ref,
    big_ref,
    small_ref,
    state_in,
    cot_in,
    land_ref,
    kern_ref,
    cb_ref,
    gain_ref,
    lb_ref,
    we_ref,
    be_ref,
    wp_ref,
    planes,
    turned,
    s_ext,
    d_ext,
    wet16,
    x_ref,
    norm_ref,
    rstd_ref,
    zed_ref,
    pre_ref,
    dact_ref,
    act_ref,
    dhid_ref,
    taps_ref,
    wbd,
    wpbd,
    mean_ref,
    mean2_ref,
    eg_ref,
    pg_ref,
    acc_ref,
    tap_out,
    pay_b,
    part_b,
    gather_b,
    pay_s,
    part_s,
    gather_s,
    row_send,
    row_recv,
    col_send,
    col_recv,
    hello_sem,
    in_sem,
    row_ssem,
    row_rsem,
    col_ssem,
    col_rsem,
    sb1,
    rb1,
    sb2,
    rb2,
    sb3,
    rb3,
    ss1,
    rs1,
    ss2,
    rs2,
    ss3,
    rs3,
):
    la = lax.axis_index("lat")
    lo = lax.axis_index("lon")
    east = lax.rem(lo + 1, N_GROUP)
    west = lax.rem(lo + N_GROUP - 1, N_GROUP)
    has_north = la > 0
    has_south = la < N_GROUP - 1

    inputs = [
        pltpu.make_async_copy(src, dst, in_sem.at[i])
        for i, (src, dst) in enumerate(
            (
                (state_hbm, state_in),
                (cot_hbm, cot_in),
                (land_hbm, land_ref),
                (kern_hbm, kern_ref),
                (cb_hbm, cb_ref),
                (gain_hbm, gain_ref),
                (lb_hbm, lb_ref),
                (we_hbm, we_ref),
                (be_hbm, be_ref),
                (wp_hbm, wp_ref),
            )
        )
    ]
    for copy in inputs:
        copy.start()

    def lat_peer(k):
        return {"lat": lax.rem(la + k, N_GROUP), "lon": lo}

    def lon_peer(k):
        return {"lat": la, "lon": lax.rem(lo + k, N_GROUP)}

    barrier = pltpu.get_barrier_semaphore()
    for k in (1, N_GROUP - 1):
        pl.semaphore_signal(barrier, inc=1, device_id=lat_peer(k), device_id_type=MESH)
        pl.semaphore_signal(barrier, inc=1, device_id=lon_peer(k), device_id_type=MESH)
    for side in (east, west):

        @pl.when(has_north)
        def _():
            pl.semaphore_signal(
                barrier, inc=1, device_id={"lat": la - 1, "lon": side}, device_id_type=MESH
            )

        @pl.when(has_south)
        def _():
            pl.semaphore_signal(
                barrier, inc=1, device_id={"lat": la + 1, "lon": side}, device_id_type=MESH
            )

    def hello(n):
        for k in (2**n, N_GROUP - 2**n):
            pl.semaphore_signal(
                hello_sem.at[0, n], inc=1, device_id=lat_peer(k), device_id_type=MESH
            )
            pl.semaphore_signal(
                hello_sem.at[1, n], inc=1, device_id=lon_peer(k), device_id_type=MESH
            )

    def heard(n):
        pl.semaphore_wait(hello_sem.at[0, n], 2)
        pl.semaphore_wait(hello_sem.at[1, n], 2)

    lane = lax.broadcasted_iota(jnp.int32, (ROWS, 8, 128), 2)
    sub = lax.broadcasted_iota(jnp.int32, (ROWS, 8, 128), 1)

    s_ext[:, 136:144, :] = jnp.zeros((EXT_ROWS, 8, 128), f32)
    d_ext[:, 136:144, :] = jnp.zeros((EXT_ROWS, 8, 128), f32)
    for ref in (s_ext, d_ext):

        @pl.when(jnp.logical_not(has_north))
        def _():
            ref[0:3] = jnp.zeros((3, EXT_COLS, 128), f32)

        @pl.when(jnp.logical_not(has_south))
        def _():
            ref[11:14] = jnp.zeros((3, EXT_COLS, 128), f32)

    planes[2] = jnp.zeros((CHAN * ROWS, 128), f32)

    def to_planes(load):
        def step(i, carry):
            at = pl.ds(pl.multiple_of(i * 8, 8), 8)
            x = load(at)
            to = pl.ds(pl.multiple_of(i * 64, 64), 64)
            planes[0, to, :] = x[:, :, 0:128].reshape(64, 128)
            planes[1, to, :] = x[:, :, 128:256].reshape(64, 128)
            planes[2, to, 0:14] = x[:, :, 256:270].reshape(64, 14)
            return carry

        lax.fori_loop(0, 8, step, 0)

    def fold(x):
        return jnp.sum(x.reshape(-1, 8, x.shape[-1]), axis=0)

    half_lane = lax.broadcasted_iota(jnp.int32, (PITCH, 128), 1) < 64

    def turn_in(put):
        def step(p, carry):
            r = p * 2
            for k in range(3):
                both = jnp.concatenate(
                    [
                        planes[k, pl.ds(r, CHAN, stride=ROWS), :],
                        planes[k, pl.ds(r + 1, CHAN, stride=ROWS), :],
                    ],
                    axis=0,
                )
                turned[128 * k : 128 * k + 128, :] = both.astype(bf16).T.astype(f32)
            h0 = turned[0:PITCH, :]
            h1 = turned[HALF : HALF + PITCH, :]
            put(
                r,
                jnp.where(half_lane, h0, pltpu.roll(h1, 64, axis=1)),
                jnp.where(half_lane, pltpu.roll(h0, 64, axis=1), h1),
            )
            return carry

        lax.fori_loop(0, ROWS // 2, step, 0)

    def exchange(ext, n):
        to_east = pltpu.roll(ext[3:11, 135:143, :], 64, axis=2)
        to_west = pltpu.roll(ext[3:11, 1:9, :], 64, axis=2)
        col_send[n, 0] = to_east
        col_send[n, 1] = to_west
        ext[3:11, 0:8, :] = jnp.where((sub < 3) & (lane >= 64), to_east, ext[3:11, 0:8, :])
        ext[3:11, 136:144, :] = jnp.where(
            (sub >= 2) & (sub < 5) & (lane < 64), to_west, ext[3:11, 136:144, :]
        )
        row_send[n, 0] = ext[3:6].astype(bf16)
        row_send[n, 1] = ext[8:11].astype(bf16)

    def rows_copy(n, way):
        return pltpu.make_async_remote_copy(
            src_ref=row_send.at[n, way],
            dst_ref=row_recv.at[n, way],
            send_sem=row_ssem.at[n, way],
            recv_sem=row_rsem.at[n, way],
            device_id={"lat": la - 1 + 2 * way, "lon": lo},
            device_id_type=MESH,
        )

    def cols_copy(n, way, turn):
        src = col_send.at[n, way]
        dst = col_recv.at[n, way]
        if turn == 1:
            src, dst = src.at[0:3], dst.at[11:14]
        elif turn == 2:
            src, dst = src.at[5:8], dst.at[0:3]
        else:
            dst = dst.at[3:11]
        return pltpu.make_async_remote_copy(
            src_ref=src,
            dst_ref=dst,
            send_sem=col_ssem.at[n, way, turn],
            recv_sem=col_rsem.at[n, way, turn],
            device_id={
                "lat": la + (0, -1, 1)[turn],
                "lon": (east, west)[way],
            },
            device_id_type=MESH,
        )

    def start_copies(n):
        @pl.when(has_north)
        def _():
            rows_copy(n, 0).start()
            cols_copy(n, 0, 1).start()
            cols_copy(n, 1, 1).start()

        @pl.when(has_south)
        def _():
            rows_copy(n, 1).start()
            cols_copy(n, 0, 2).start()
            cols_copy(n, 1, 2).start()

        cols_copy(n, 0, 0).start()
        cols_copy(n, 1, 0).start()

    def finish_copies(ext, n):
        @pl.when(has_north)
        def _():
            rows_copy(n, 0).wait_send()
            cols_copy(n, 0, 1).wait_send()
            cols_copy(n, 1, 1).wait_send()
            rows_copy(n, 1).wait_recv()
            cols_copy(n, 0, 2).wait_recv()
            cols_copy(n, 1, 2).wait_recv()
            ext[0:3] = row_recv[n, 1].astype(f32)

        @pl.when(has_south)
        def _():
            rows_copy(n, 1).wait_send()
            cols_copy(n, 0, 2).wait_send()
            cols_copy(n, 1, 2).wait_send()
            rows_copy(n, 0).wait_recv()
            cols_copy(n, 0, 1).wait_recv()
            cols_copy(n, 1, 1).wait_recv()
            ext[11:14] = row_recv[n, 0].astype(f32)

        cols_copy(n, 0, 0).wait()
        cols_copy(n, 1, 0).wait()

        def fill(first, last):
            from_west = col_recv[n, 0, first:last]
            from_east = col_recv[n, 1, first:last]
            m = last - first
            ext[first:last, 0:8, :] = jnp.where(
                (sub[:m] < 3) & (lane[:m] < 64), from_west, ext[first:last, 0:8, :]
            )
            ext[first:last, 136:144, :] = jnp.where(
                (sub[:m] >= 2) & (sub[:m] < 5) & (lane[:m] >= 64),
                from_east,
                ext[first:last, 136:144, :],
            )

        fill(3, 11)

        @pl.when(has_north)
        def _():
            fill(0, 3)

        @pl.when(has_south)
        def _():
            fill(11, 14)

    def convolve(ext, flip, bias, tiles, stride, part=0, unroll=1):
        def one(t):
            at = pl.multiple_of(t * (8 * stride) + 8 * (stride == 1), 8)
            if part == 2:
                acc = [x_ref[pl.ds(at + r * PITCH, 8), :] for r in range(ROWS)]
            else:
                first = jnp.zeros((8, 128), f32)
                if bias is not None:
                    first = first + bias
                acc = [first] * ROWS
            for b in range(TAPS):
                rows = {
                    i: ext[i, pl.ds(at + b, 8), :]
                    for i in range(EXT_ROWS)
                    if part == 0 or (part == 1) == (3 <= i < 11)
                }
                for a in range(TAPS):
                    i = a * TAPS + b
                    tap = taps_ref[48 - i if flip else i]
                    for r in range(ROWS):
                        if r + a in rows:
                            acc[r] = acc[r] + tap * rows[r + a]
            for r in range(ROWS):
                x_ref[pl.ds(at + r * PITCH, 8), :] = acc[r]

        def step(t, carry):
            for u in range(unroll):
                one(t * unroll + u)
            return carry

        lax.fori_loop(0, tiles // unroll, step, 0)

    inputs[0].wait()
    to_planes(lambda at: state_in[at].astype(f32))

    def put_state(r, one, two):
        s_ext[r + 3, 3 : 3 + PITCH, :] = one
        s_ext[r + 4, 3 : 3 + PITCH, :] = two

    turn_in(put_state)
    exchange(s_ext, 0)
    pl.semaphore_wait(
        barrier,
        4
        + 2 * has_north.astype(jnp.int32)
        + 2 * has_south.astype(jnp.int32),
    )
    start_copies(0)
    hello(0)

    inputs[1].wait()
    inputs[2].wait()
    land = land_ref[...].astype(f32)
    to_planes(lambda at: cot_in[at].astype(f32) * land[None])

    acc_ref[...] = jnp.zeros((5, 8, 512), f32)
    own = lax.broadcasted_iota(jnp.int32, (PITCH, 128), 0) < HALF

    def put_wet(r, one, two):
        both = jnp.concatenate([jnp.where(own, one, 0.0), jnp.where(own, two, 0.0)], axis=0)
        wet16[pl.ds(pl.multiple_of(r * PITCH, STEP), STEP), :] = both.astype(bf16)
        acc_ref[0, :, 0:128] += fold(both)

    turn_in(put_wet)

    for copy in inputs[3:]:
        copy.wait()
    for a in range(TAPS):
        for b in range(TAPS):
            one = kern_ref[a, b : b + 1, :]
            taps_ref[a * TAPS + b] = jnp.broadcast_to(
                jnp.concatenate([one, one], axis=1), (8, 128)
            )
    wbd[...] = jnp.zeros((128, 512), bf16)
    wbd[0:64, 0:256] = we_ref[...]
    wbd[64:128, 256:512] = we_ref[...]
    wpbd[...] = jnp.zeros((128, 512), bf16)
    wpbd[0:64, 0:256] = wp_ref[...]
    wpbd[64:128, 256:512] = wp_ref[...]
    at_row = lax.broadcasted_iota(jnp.int32, (256, 256), 0) // 64
    at_col = lax.broadcasted_iota(jnp.int32, (256, 256), 1) // 64
    mean2_ref[...] = jnp.where(at_row == at_col, 1.0 / CHAN, 0.0).astype(bf16)
    mean_ref[0:128, :] = mean2_ref[0:128, 0:128]
    mean_ref[128:256, :] = mean2_ref[0:128, 0:128]

    def twice(ref):
        return jnp.concatenate([ref[...], ref[...]], axis=1)

    conv_bias = twice(cb_ref)
    gain = twice(gain_ref)
    ln_bias = twice(lb_ref)
    be = twice(be_ref)

    heard(0)
    hello(1)

    def back(q, carry):
        at = pl.ds(pl.multiple_of(q * STEP, STEP), STEP)
        dact_ref[at, :] = dot(wet16[at, :], wpbd[...], NN)
        return carry

    lax.fori_loop(0, CELLS // STEP, back, 0)
    convolve(s_ext, False, conv_bias, TILES - 2, 1, 1, UA)
    heard(1)
    hello(2)
    finish_copies(s_ext, 0)
    convolve(s_ext, False, conv_bias, TILES - 2, 1, 2, UB)
    convolve(s_ext, False, conv_bias, 2, TILES - 1, 0, UE)

    def forward(q, carry):
        at = pl.ds(pl.multiple_of(q * PART, PART), PART)
        x = x_ref[at, :]
        cen = x - dot(split(x), mean_ref[...], NN)
        var = dot((cen * cen).astype(bf16), mean_ref[0:128, :], NN)
        rstd = lax.rsqrt(var + ln_eps)
        normed = cen * rstd
        zed = (normed * gain + ln_bias).astype(bf16)
        norm_ref[at, :] = normed
        rstd_ref[at, :] = rstd
        zed_ref[at, :] = zed
        pre_ref[at, :] = dot(zed, wbd[...], NN)
        return carry

    lax.fori_loop(0, CELLS // PART, forward, 0)

    def gelu(i, total):
        rows = pl.ds(pl.multiple_of(i * GROUP, GROUP), GROUP)
        for k in range(4):
            cols = slice(128 * k, 128 * k + 128)
            pre = pre_ref[rows, cols] + be[:, cols]
            grow = jnp.exp2(pre * pre * half_log2e)
            phi = 0.5 + 0.5 * lax.erf(pre * root_half)
            slope = phi + pre * grow * inv_root_tau
            act_ref[rows, cols] = (pre * phi).astype(bf16)
            dhid = (dact_ref[rows, cols] * slope).astype(bf16)
            dhid_ref[rows, cols] = dhid
            acc_ref[1, :, cols] += fold(dhid.astype(f32))
        return total

    lax.fori_loop(0, CELLS // GROUP, gelu, 0)

    def backward(q, carry):
        at = pl.ds(pl.multiple_of(q * BACK, BACK), BACK)
        dzed = dot(dhid_ref[at, :], wbd[...], NT)
        normed = norm_ref[at, :]
        acc_ref[2, :, 0:128] += fold(dzed * normed)
        acc_ref[3, :, 0:128] += fold(dzed)
        dnorm = dzed * gain
        both = jnp.concatenate([dnorm.astype(bf16), (dnorm * normed).astype(bf16)], axis=1)
        means = dot(both, mean2_ref[...], NN)
        dconv = rstd_ref[at, :] * (dnorm - means[:, 0:128] - normed * means[:, 128:256])
        x_ref[at, :] = dconv
        acc_ref[4, :, 0:128] += fold(dconv)
        return carry

    eg_ref[...] = dot(zed_ref[...], dhid_ref[...], TN)
    pg_ref[...] = dot(wet16[...], act_ref[...], TN)
    backward(0, 0)

    def halves(x):
        return x + pltpu.roll(x, 64, axis=1)

    for i in range(N_GROUP):
        c, e = 8 * (i // 2), 128 * (i % 2)
        one, two = [
            ref[c : c + 8, e : e + 128] + ref[64 + c : 72 + c, 256 + e : 384 + e]
            for ref in (eg_ref, pg_ref)
        ]
        pay_b[i] = jnp.concatenate([one, two], axis=0).astype(bf16)

    def scatter(pay, part, ssem, rsem):
        copies = []
        for k in range(1, N_GROUP):
            copies.append(
                pltpu.make_async_remote_copy(
                    src_ref=pay.at[lax.rem(la + k, N_GROUP)],
                    dst_ref=part.at[k],
                    send_sem=ssem.at[k],
                    recv_sem=rsem.at[k],
                    device_id=lat_peer(k),
                    device_id_type=MESH,
                )
            )
            copies[-1].start()
        return copies

    def spread(ref, at, peer, ssem, rsem):
        copies = []
        for k in range(1, N_GROUP):
            copies.append(
                pltpu.make_async_remote_copy(
                    src_ref=ref.at[at],
                    dst_ref=ref.at[at],
                    send_sem=ssem.at[k],
                    recv_sem=rsem.at[k],
                    device_id=peer(k),
                    device_id_type=MESH,
                )
            )
            copies[-1].start()
        return copies

    def scattered(pay, part, gather, copies):
        total = pay[la].astype(f32)
        for k in range(1, N_GROUP):
            copies[k - 1].wait()
            total = total + part[k].astype(f32)
        gather[lo] = total.astype(gather.dtype)

    scale = 1.0 / math.sqrt(ROWS * N_GROUP * COLS * N_GROUP)

    def gathered(gather, out, copies):
        for copy in copies:
            copy.wait()
        total = gather[0].astype(f32)
        for k in range(1, N_GROUP):
            total = total + gather[k].astype(f32)
        out[la] = (total * scale).astype(out.dtype)

    heard(2)
    copies_b = scatter(pay_b, part_b, sb1, rb1)
    def place(r, carry):
        d_ext[r + 3, 3 : 3 + PITCH, :] = x_ref[pl.ds(pl.multiple_of(r * PITCH, 8), PITCH), :]
        return carry

    lax.fori_loop(0, ROWS, place, 0)
    exchange(d_ext, 1)
    start_copies(1)

    for group in ((0, 1, 2), (3, 4), (5, 6)):

        def tap_step(t, acc):
            at = pl.multiple_of(t * 8, 8)
            d = [x_ref[pl.ds(at + r * PITCH, 8), :] for r in range(ROWS)]
            new = list(acc)
            for n, b in enumerate(group):
                for i in range(EXT_ROWS):
                    x = s_ext[i, pl.ds(at + b, 8), :]
                    for a in range(TAPS):
                        if 0 <= i - a < ROWS:
                            new[n * TAPS + a] = new[n * TAPS + a] + d[i - a] * x
            return tuple(new)

        zero = jnp.zeros((8, 128), f32)
        acc = lax.fori_loop(0, TILES, tap_step, (zero,) * (TAPS * len(group)))
        for n, b in enumerate(group):
            for a in range(TAPS):
                tap_out[a * TAPS + b] = acc[n * TAPS + a]

    first_half = lax.broadcasted_iota(jnp.int32, (1, 128), 1) < 64

    def sums_of(x):
        return halves(jnp.sum(x, axis=0, keepdims=True))

    rows = []
    for i in range(25):
        one = sums_of(tap_out[i])
        two = sums_of(tap_out[25 + i]) if i < 24 else jnp.zeros((1, 128), f32)
        rows.append(jnp.where(first_half, one, two))
    wide = jnp.sum(acc_ref[1], axis=0, keepdims=True)
    wide = wide[:, 0:256] + wide[:, 256:512]
    rows.append(wide[:, 0:128])
    rows.append(wide[:, 128:256])
    rows.append(
        jnp.where(first_half, sums_of(acc_ref[4, :, 0:128]), sums_of(acc_ref[2, :, 0:128]))
    )
    rows.append(
        jnp.where(first_half, sums_of(acc_ref[3, :, 0:128]), sums_of(acc_ref[0, :, 0:128]))
    )
    while len(rows) < 32:
        rows.append(jnp.zeros((1, 128), f32))
    for i in range(N_GROUP):
        pay_s[i, 0:1, :] = rows[2 * i]
        pay_s[i, 1:2, :] = rows[2 * i + 1]

    copies_s = scatter(pay_s, part_s, ss1, rs1)

    scattered(pay_b, part_b, gather_b, copies_b)
    copies_b = spread(gather_b, lo, lon_peer, sb2, rb2)
    scattered(pay_s, part_s, gather_s, copies_s)
    copies_s = spread(gather_s, lo, lon_peer, ss2, rs2)

    finish_copies(d_ext, 1)
    convolve(d_ext, True, None, 1, TILES)
    convolve(d_ext, True, None, TILES - 1, 1)
    gathered(gather_b, big_ref, copies_b)
    copies_b = spread(big_ref, la, lat_peer, sb3, rb3)

    def turn_out(p, carry):
        r = p * 2
        g0 = x_ref[pl.ds(pl.multiple_of(r * PITCH, 8), PITCH), :]
        g1 = x_ref[pl.ds(pl.multiple_of(r * PITCH + PITCH, 8), PITCH), :]
        turned[0:PITCH, :] = jnp.where(half_lane, g0, pltpu.roll(g1, 64, axis=1))
        turned[HALF : HALF + PITCH, :] = jnp.where(half_lane, pltpu.roll(g0, 64, axis=1), g1)
        for k in range(3):
            back = turned[128 * k : 128 * k + 128, :].T
            planes[k, pl.ds(r, CHAN, stride=ROWS), :] = back[0:64]
            planes[k, pl.ds(r + 1, CHAN, stride=ROWS), :] = back[64:128]
        return carry

    lax.fori_loop(0, ROWS // 2, turn_out, 0)

    def write_out(i, carry):
        at = pl.ds(pl.multiple_of(i * 8, 8), 8)
        of = pl.ds(pl.multiple_of(i * 64, 64), 64)
        for k in range(3):
            cols = slice(128 * k, min(128 * k + 128, COLS))
            width = cols.stop - cols.start
            value = planes[k, of, 0:width].reshape(8, 8, width)
            grad_ref[at, :, cols] = (cot_in[at, :, cols].astype(f32) + value).astype(bf16)
        return carry

    lax.fori_loop(0, 8, write_out, 0)

    gathered(gather_s, small_ref, copies_s)
    copies_s = spread(small_ref, la, lat_peer, ss3, rs3)
    for copy in copies_b + copies_s:
        copy.wait()


def finish(grad_ref, big_ref, small_ref, *refs):
    outs, staged, sems = refs[0:9], refs[9:17], refs[17]
    kern_out, cb_out, gain_out, lb_out, expand_out, be_out, project_out, bp_out = staged
    copies = [
        pltpu.make_async_copy(src, dst, sems.at[i])
        for i, (src, dst) in enumerate(zip((grad_ref,) + tuple(staged), outs))
    ]
    copies[0].start()
    for i in range(N_GROUP):
        c, e = 8 * (i // 2), 128 * (i % 2)
        both = big_ref[i].astype(f32)
        expand_out[c : c + 8, e : e + 128] = both[0:8]
        project_out[c : c + 8, e : e + 128] = both[8:16]
    copies[5].start()
    copies[7].start()

    def row(i):
        return small_ref[i // 2, i % 2 : i % 2 + 1, :]

    def turned(i):
        return pltpu.roll(row(i), 64, axis=1)

    for i in range(TAPS * TAPS):
        a, b = i // TAPS, i % TAPS
        kern_out[a, b : b + 1, :] = (row(i) if i < 25 else turned(i - 25))[:, 0:64]
    copies[1].start()
    cb_out[...] = row(27)[:, 0:64]
    gain_out[...] = turned(27)[:, 0:64]
    lb_out[...] = row(28)[:, 0:64]
    be_out[:, 0:128] = row(25)
    be_out[:, 128:256] = row(26)
    bp_out[...] = turned(28)[:, 0:64]
    for i in (2, 3, 4, 6, 8):
        copies[i].start()
    for copy in copies:
        copy.wait()


def far(x):
    return pltpu.with_memory_space_constraint(x, pltpu.HBM)


def body(
    state, land_sea, cotangent, kernel, conv_bias, ln_gain, ln_bias, w_expand, b_expand, w_project
):
    vmem = pl.BlockSpec(memory_space=pltpu.VMEM)
    hbm = pl.BlockSpec(memory_space=pltpu.HBM)
    sds = jax.ShapeDtypeStruct
    sem = pltpu.SemaphoreType.DMA
    big = (N_GROUP, 16, 128)
    small = (N_GROUP, 2, 128)
    grad, big_sums, small_sums = pl.pallas_call(
        kernel_body,
        out_shape=(
            sds((CHAN, ROWS, COLS), bf16),
            sds(big, bf16),
            sds(small, f32),
        ),
        in_specs=[hbm] * 10,
        out_specs=(vmem, vmem, vmem),
        scratch_shapes=[
            pltpu.VMEM((CHAN, ROWS, COLS), bf16),
            pltpu.VMEM((CHAN, ROWS, COLS), bf16),
            pltpu.VMEM((ROWS, COLS), jnp.int32),
            pltpu.VMEM((TAPS, TAPS, CHAN), f32),
            pltpu.VMEM((1, CHAN), f32),
            pltpu.VMEM((1, CHAN), f32),
            pltpu.VMEM((1, CHAN), f32),
            pltpu.VMEM((CHAN, EXPAND), bf16),
            pltpu.VMEM((1, EXPAND), f32),
            pltpu.VMEM((CHAN, EXPAND), bf16),
            pltpu.VMEM((3, CHAN * ROWS, 128), f32),
            pltpu.VMEM((384, 128), f32),
            pltpu.VMEM((EXT_ROWS, EXT_COLS, 128), f32),
            pltpu.VMEM((EXT_ROWS, EXT_COLS, 128), f32),
            pltpu.VMEM((CELLS, 128), bf16),
            pltpu.VMEM((CELLS, 128), f32),
            pltpu.VMEM((CELLS, 128), f32),
            pltpu.VMEM((CELLS, 128), f32),
            pltpu.VMEM((CELLS, 128), bf16),
            pltpu.VMEM((CELLS, 512), f32),
            pltpu.VMEM((CELLS, 512), f32),
            pltpu.VMEM((CELLS, 512), bf16),
            pltpu.VMEM((CELLS, 512), bf16),
            pltpu.VMEM((TAPS * TAPS, 8, 128), f32),
            pltpu.VMEM((128, 512), bf16),
            pltpu.VMEM((128, 512), bf16),
            pltpu.VMEM((256, 128), bf16),
            pltpu.VMEM((256, 256), bf16),
            pltpu.VMEM((128, 512), f32),
            pltpu.VMEM((128, 512), f32),
            pltpu.VMEM((5, 8, 512), f32),
            pltpu.VMEM((TAPS * TAPS, 8, 128), f32),
            pltpu.VMEM(big, bf16),
            pltpu.VMEM(big, bf16),
            pltpu.VMEM(big, bf16),
            pltpu.VMEM(small, f32),
            pltpu.VMEM(small, f32),
            pltpu.VMEM(small, f32),
            pltpu.VMEM((2, 2, 3, EXT_COLS, 128), bf16),
            pltpu.VMEM((2, 2, 3, EXT_COLS, 128), bf16),
            pltpu.VMEM((2, 2, ROWS, 8, 128), f32),
            pltpu.VMEM((2, 2, EXT_ROWS, 8, 128), f32),
            pltpu.SemaphoreType.REGULAR((2, 3)),
            sem((10,)),
            sem((2, 2)),
            sem((2, 2)),
            sem((2, 2, 3)),
            sem((2, 2, 3)),
        ]
        + [sem((N_GROUP,))] * 12,
        compiler_params=pltpu.CompilerParams(
            collective_id=0, has_side_effects=True, vmem_limit_bytes=48 * 2**20
        ),
    )(
        *map(
            far,
            (
                state,
                cotangent,
                land_sea,
                kernel.transpose(1, 2, 0),
                conv_bias[None],
                ln_gain[None],
                ln_bias[None],
                w_expand,
                b_expand[None],
                w_project.T,
            ),
        )
    )
    outs = pl.pallas_call(
        finish,
        out_shape=(
            sds((CHAN, ROWS, COLS), bf16),
            sds((TAPS, TAPS, CHAN), f32),
            sds((1, CHAN), f32),
            sds((1, CHAN), f32),
            sds((1, CHAN), f32),
            sds((CHAN, EXPAND), f32),
            sds((1, EXPAND), f32),
            sds((CHAN, EXPAND), f32),
            sds((1, CHAN), f32),
        ),
        in_specs=[vmem] * 3,
        out_specs=(hbm,) * 9,
        scratch_shapes=[
            pltpu.VMEM((TAPS, TAPS, CHAN), f32),
            pltpu.VMEM((1, CHAN), f32),
            pltpu.VMEM((1, CHAN), f32),
            pltpu.VMEM((1, CHAN), f32),
            pltpu.VMEM((CHAN, EXPAND), f32),
            pltpu.VMEM((1, EXPAND), f32),
            pltpu.VMEM((CHAN, EXPAND), f32),
            pltpu.VMEM((1, CHAN), f32),
            sem((9,)),
        ],
        compiler_params=pltpu.CompilerParams(vmem_limit_bytes=8 * 2**20),
    )(grad, big_sums, small_sums)
    outs = list(outs)
    outs[1] = outs[1].transpose(2, 0, 1)
    outs[7] = outs[7].T
    for i in (2, 3, 4, 6, 8):
        outs[i] = outs[i].reshape(-1)
    return tuple(outs)


def solution(mesh):
    in_specs = (
        P(None, "lat", "lon"),
        P("lat", "lon"),
        P(None, "lat", "lon"),
        P(),
        P(),
        P(),
        P(),
        P(),
        P(),
        P(),
    )
    out_specs = (P(None, "lat", "lon"), P(), P(), P(), P(), P(), P(), P(), P())
    return jax.shard_map(body, mesh=mesh, in_specs=in_specs, out_specs=out_specs, check_vma=False)
```

profile of v0, /device:TPU:1, one launch (start us, length us, event | category | flops | bytes accessed | tf_op | source)
XLA Modules:
  0.0 40.0 jit_solution(281775306015695732)
XLA Ops:
  0.6 38.5 %shard_map.169 = (bf16[64,8,270]{2,1,0:T(8,128)(2,1)S(1)}, bf16[16,16,128]{2,1,0:T(8,128)(2,1)S(1)}, f32[16,2,128]{2,1,0:T(2,128)S(1)}) custom-call(bf16[64,8,270]{2,1,0:T(8,128)(2,1)} %state_hbm.1, bf16[64,8,270]{2,1,0:T(8,128)(2,1)} %cot_hbm.1, s32[8,270]{1,0:T(8,128)} %land_hbm.1, f32[7,7,64]{2,1,0:T(8,128)} %bitcast.14, f32[1,64]{1,0:T(1,128)} %bitcast.16, ...), custom_call_target="tpu_custom_call" | custom-call | tf_op jit(solution)/shard_map/pallas_call | solution.py:728
  39.1 0.9 %shard_map.170 = (bf16[64,8,270]{2,1,0:T(8,128)(2,1)}, f32[7,7,64]{2,1,0:T(8,128)}, f32[1,64]{1,0:T(1,128)}, f32[1,64]{1,0:T(1,128)}, f32[1,64]{1,0:T(1,128)}, /...) custom-call(bf16[64,8,270]{2,1,0:T(8,128)(2,1)S(1)} %get-tuple-element.21.grad_ref, ...), custom_call_target="tpu_custom_call" | custom-call | tf_op jit(solution)/shard_map/pallas_call | solution.py:808
where the time goes:
time: 40.1 us; the launch traced here: 40 us
  Pallas kernels  39.4 us (98%)
  between operations  0.65 us (2%)
    pallas_call x1, Pallas kernels, body(): pl.pallas_call(kernel_body, out_shape=(sds((CHAN, ROWS, COLS), bf16), sds...  38.5 us
    pallas_call x1, Pallas kernels, body(): pl.pallas_call(finish, out_shape=(sds((CHAN, ROWS, COLS), bf16), sds((TAP...  0.88 us

commit v1 on v0

--- a/solution.py
+++ b/solution.py
@@ -23,6 +23,8 @@
 GROUP = 272
 BACK = 1088
 UA = 3
+UT = 4
+GROUPS = ((0, 1, 2, 3), (4, 5, 6))
 UB = 5
 UE = 2
 N_GROUP = 16
@@ -513,9 +515,6 @@
     pg_ref[...] = dot(wet16[...], act_ref[...], TN)
     backward(0, 0)
 
-    def halves(x):
-        return x + pltpu.roll(x, 64, axis=1)
-
     for i in range(N_GROUP):
         c, e = 8 * (i // 2), 128 * (i % 2)
         one, two = [
@@ -583,10 +582,10 @@
     exchange(d_ext, 1)
     start_copies(1)
 
-    for group in ((0, 1, 2), (3, 4), (5, 6)):
-
-        def tap_step(t, acc):
-            at = pl.multiple_of(t * 8, 8)
+    for group in GROUPS:
+
+        def tap_tile(t, acc):
+            at = t * 8 if isinstance(t, int) else pl.multiple_of(t * 8, 8)
             d = [x_ref[pl.ds(at + r * PITCH, 8), :] for r in range(ROWS)]
             new = list(acc)
             for n, b in enumerate(group):
@@ -597,32 +596,34 @@
                             new[n * TAPS + a] = new[n * TAPS + a] + d[i - a] * x
             return tuple(new)
 
+        def tap_step(t, acc):
+            for u in range(UT):
+                acc = tap_tile(t * UT + 1 + u, acc)
+            return acc
+
         zero = jnp.zeros((8, 128), f32)
-        acc = lax.fori_loop(0, TILES, tap_step, (zero,) * (TAPS * len(group)))
+        acc = tap_tile(0, (zero,) * (TAPS * len(group)))
+        acc = lax.fori_loop(0, (TILES - 1) // UT, tap_step, acc)
         for n, b in enumerate(group):
             for a in range(TAPS):
                 tap_out[a * TAPS + b] = acc[n * TAPS + a]
 
-    first_half = lax.broadcasted_iota(jnp.int32, (1, 128), 1) < 64
-
-    def sums_of(x):
-        return halves(jnp.sum(x, axis=0, keepdims=True))
-
-    rows = []
-    for i in range(25):
-        one = sums_of(tap_out[i])
-        two = sums_of(tap_out[25 + i]) if i < 24 else jnp.zeros((1, 128), f32)
-        rows.append(jnp.where(first_half, one, two))
+    first_half = lax.broadcasted_iota(jnp.int32, (8, 128), 1) < 64
+
+    def pair(one, two):
+        both = jnp.where(first_half, one, two)
+        return jnp.sum(
+            both + pltpu.roll(jnp.where(first_half, two, one), 64, axis=1), axis=0, keepdims=True
+        )
+
+    blank = jnp.zeros((8, 128), f32)
+    rows = [pair(tap_out[i], tap_out[25 + i] if i < 24 else blank) for i in range(25)]
     wide = jnp.sum(acc_ref[1], axis=0, keepdims=True)
     wide = wide[:, 0:256] + wide[:, 256:512]
     rows.append(wide[:, 0:128])
     rows.append(wide[:, 128:256])
-    rows.append(
-        jnp.where(first_half, sums_of(acc_ref[4, :, 0:128]), sums_of(acc_ref[2, :, 0:128]))
-    )
-    rows.append(
-        jnp.where(first_half, sums_of(acc_ref[3, :, 0:128]), sums_of(acc_ref[0, :, 0:128]))
-    )
+    rows.append(pair(acc_ref[4, :, 0:128], acc_ref[2, :, 0:128]))
+    rows.append(pair(acc_ref[3, :, 0:128], acc_ref[0, :, 0:128]))
     while len(rows) < 32:
         rows.append(jnp.zeros((1, 128), f32))
     for i in range(N_GROUP):

time: 40.1 us -> 39.7 us (0.990)
  no operation moved by 1% of the time
where the time goes in v1:
time: 39.7 us; the launch traced here: 39.6 us
  Pallas kernels  39 us (98%)
  between operations  0.65 us (2%)
    pallas_call x1, Pallas kernels, body(): pl.pallas_call(kernel_body, out_shape=(sds((CHAN, ROWS, COLS), bf16), sds...  38.1 us
    pallas_call x1, Pallas kernels, body(): pl.pallas_call(finish, out_shape=(sds((CHAN, ROWS, COLS), bf16), sds((TAP...  0.88 us

profile of v1, /device:TPU:1, one launch (start us, length us, event | category | flops | bytes accessed | tf_op | source)
XLA Modules:
  0.0 39.6 jit_solution(12596854869103815042)
XLA Ops:
  0.6 38.1 %shard_map.169 = (bf16[64,8,270]{2,1,0:T(8,128)(2,1)S(1)}, bf16[16,16,128]{2,1,0:T(8,128)(2,1)S(1)}, f32[16,2,128]{2,1,0:T(2,128)S(1)}) custom-call(bf16[64,8,270]{2,1,0:T(8,128)(2,1)} %state_hbm.1, bf16[64,8,270]{2,1,0:T(8,128)(2,1)} %cot_hbm.1, s32[8,270]{1,0:T(8,128)} %land_hbm.1, f32[7,7,64]{2,1,0:T(8,128)} %bitcast.14, f32[1,64]{1,0:T(1,128)} %bitcast.16, ...), custom_call_target="tpu_custom_call" | custom-call | tf_op jit(solution)/shard_map/pallas_call | solution.py:729
  38.7 0.9 %shard_map.170 = (bf16[64,8,270]{2,1,0:T(8,128)(2,1)}, f32[7,7,64]{2,1,0:T(8,128)}, f32[1,64]{1,0:T(1,128)}, f32[1,64]{1,0:T(1,128)}, f32[1,64]{1,0:T(1,128)}, /...) custom-call(bf16[64,8,270]{2,1,0:T(8,128)(2,1)S(1)} %get-tuple-element.21.grad_ref, ...), custom_call_target="tpu_custom_call" | custom-call | tf_op jit(solution)/shard_map/pallas_call | solution.py:809

commit v2 on v1

--- a/solution.py
+++ b/solution.py
@@ -23,7 +23,7 @@
 GROUP = 272
 BACK = 1088
 UA = 3
-UT = 4
+UT = 8
 GROUPS = ((0, 1, 2, 3), (4, 5, 6))
 UB = 5
 UE = 2

time: 39.7 us -> 39.7 us (level)
  no operation moved by 1% of the time
where the time goes in v2:
time: 39.7 us; the launch traced here: 39.6 us
  Pallas kernels  38.9 us (98%)
  between operations  0.65 us (2%)
    pallas_call x1, Pallas kernels, body(): pl.pallas_call(kernel_body, out_shape=(sds((CHAN, ROWS, COLS), bf16), sds...  38.1 us
    pallas_call x1, Pallas kernels, body(): pl.pallas_call(finish, out_shape=(sds((CHAN, ROWS, COLS), bf16), sds((TAP...  0.88 us

profile of v2, /device:TPU:1, one launch (start us, length us, event | category | flops | bytes accessed | tf_op | source)
XLA Modules:
  0.0 39.6 jit_solution(14183891060628541822)
XLA Ops:
  0.6 38.1 %shard_map.169 = (bf16[64,8,270]{2,1,0:T(8,128)(2,1)S(1)}, bf16[16,16,128]{2,1,0:T(8,128)(2,1)S(1)}, f32[16,2,128]{2,1,0:T(2,128)S(1)}) custom-call(bf16[64,8,270]{2,1,0:T(8,128)(2,1)} %state_hbm.1, bf16[64,8,270]{2,1,0:T(8,128)(2,1)} %cot_hbm.1, s32[8,270]{1,0:T(8,128)} %land_hbm.1, f32[7,7,64]{2,1,0:T(8,128)} %bitcast.14, f32[1,64]{1,0:T(1,128)} %bitcast.16, ...), custom_call_target="tpu_custom_call" | custom-call | tf_op jit(solution)/shard_map/pallas_call | solution.py:729
  38.7 0.9 %shard_map.170 = (bf16[64,8,270]{2,1,0:T(8,128)(2,1)}, f32[7,7,64]{2,1,0:T(8,128)}, f32[1,64]{1,0:T(1,128)}, f32[1,64]{1,0:T(1,128)}, f32[1,64]{1,0:T(1,128)}, /...) custom-call(bf16[64,8,270]{2,1,0:T(8,128)(2,1)S(1)} %get-tuple-element.21.grad_ref, ...), custom_call_target="tpu_custom_call" | custom-call | tf_op jit(solution)/shard_map/pallas_call | solution.py:809
